TPU v7x, 512 devices: a whole 4x4x16 slice. The times are simulated.
512 devices in a mesh: segment: 16 (over z_lo, x), dp: 8 (over y, core), mp: 4 (over z_hi).
Axes of the slice: x: 4, y: 4, z: 16 (z_hi: 4, z_lo: 4; z = z_hi * 4 + z_lo), core: 2. Of those that a mesh axis runs over, the one named last changes fastest.
Arguments:
- encoder_image_states: bfloat16 [8, 128, 8192], P('dp', 'segment'), may hold values from -6 to 6
- frozen_key_value: bfloat16 [16, 8192, 2, 1024], P('segment', 'dp', None, 'mp'), may hold values from -0.0625 to 0.0625
- adapter_down_weight: bfloat16 [16, 8192, 128], P('segment', 'mp'), may hold values from -0.0625 to 0.0625
- adapter_up_weight: bfloat16 [16, 2, 64, 1024], P('segment', None, None, 'mp'), may hold values from -0.75 to 0.75
- queries: bfloat16 [16, 8, 128, 8192], P('segment', 'dp', None, 'mp'), may hold values from -9 to 9
- cotangent: bfloat16 [16, 8, 128, 8192], P('segment', 'dp', None, 'mp'), may hold values from -1.5 to 1.5
- text_token_length: int32 [8], P('dp'), may hold values from 32 to 128
- image_tile_count: int32 [8], P('dp'), may hold values from 1 to 4
Outputs:
- grad_down: bfloat16 [16, 8192, 128], P('segment', 'mp')
- up_gradient: bfloat16 [16, 2, 64, 1024], P('segment', None, None, 'mp')
- grad_image: float32 [8, 128, 8192], P('dp', 'segment')
All inputs are finite; a program needn't handle non-finite values.
Results may differ from a plain program's by a relative error of at most 0.017.
The roundings to bfloat16 on the way count: a program that leaves them out, or rounds other values in their place, can miss the bound.
Values may be sent and summed in bfloat16 or wider, within the bound.
No kernel may reach another device: no remote copies, remote signals or barrier semaphores. Data moves between devices by JAX's collectives and lax.ppermute only.
A program may use at most 64 MiB of HBM per device.

v0:
```python
import jax
import jax.numpy as jnp
from jax import lax
from jax.sharding import PartitionSpec as P

HD = 128
TILES = 4
adapter_scale = 2.0
contract_rows = (((0,), (0,)), ((), ()))
contracted_columns = (((1,), (1,)), ((), ()))


def body(
    encoder_image_states,
    frozen_key_value,
    adapter_down_weight,
    adapter_up_weight,
    queries,
    cotangent,
    text_token_length,
    image_tile_count,
):
    samples = encoder_image_states.shape[0]
    model_width = encoder_image_states.shape[2]
    whole_img = lax.all_gather(encoder_image_states, "segment", axis=1, tiled=True)
    image_rows = whole_img.shape[1]
    flat_rows = samples * image_rows
    flat_img = whole_img.reshape(flat_rows, model_width)
    fourth_part = adapter_down_weight.shape[1]
    parallel_index = lax.axis_index("mp")
    image_fourth = lax.dynamic_slice_in_dim(flat_img, parallel_index * fourth_part, fourth_part, 1)
    lowrank_state = adapter_up_weight.shape[2]
    key_value_columns = adapter_up_weight.shape[3]
    lowrank_projection = lax.psum(
        jnp.dot(image_fourth, adapter_down_weight[0], preferred_element_type=jnp.float32), "mp"
    ).astype(jnp.bfloat16)
    adapted_weight = jnp.concatenate(
        [
            jnp.dot(
                lowrank_projection[:, :lowrank_state],
                adapter_up_weight[0, 0],
                preferred_element_type=jnp.float32,
            ),
            jnp.dot(
                lowrank_projection[:, lowrank_state:],
                adapter_up_weight[0, 1],
                preferred_element_type=jnp.float32,
            ),
        ],
        axis=1,
    )
    local_weight = frozen_key_value[0]
    full_weight = lax.all_gather(local_weight, "dp", axis=0, tiled=True).reshape(
        model_width, 2 * key_value_columns
    )
    frozen_output = jnp.dot(flat_img, full_weight, preferred_element_type=jnp.float32)
    key_value_pair = (frozen_output + adapter_scale * adapted_weight).astype(jnp.bfloat16)
    local_heads = queries.shape[3] // HD
    local_kv = key_value_columns // HD
    group_size = local_heads // local_kv
    text_rows = queries.shape[2]
    query_rows = queries[0].reshape(samples, text_rows, local_kv, group_size, HD)
    cot_rows = cotangent[0].reshape(samples, text_rows, local_kv, group_size, HD)
    key_rows = key_value_pair[:, :key_value_columns].reshape(samples, image_rows, local_kv, HD)
    value_rows = key_value_pair[:, key_value_columns:].reshape(samples, image_rows, local_kv, HD)
    key_mask = jnp.arange(image_rows, dtype=jnp.int32)[None, :] < image_tile_count[:, None] * (
        image_rows // TILES
    )
    row_mask = (
        jnp.arange(text_rows, dtype=jnp.int32)[None, :] < text_token_length[:, None]
    ).astype(jnp.float32)
    scores = jnp.einsum(
        "btgrd,bjgd->bgrtj", query_rows, key_rows, preferred_element_type=jnp.float32
    ) * HD ** (-0.5)
    masked = jnp.where(key_mask[:, None, None, None, :], scores, -1e30)
    row_top = jnp.max(masked, axis=-1, keepdims=True)
    shifted = jnp.exp(masked - row_top)
    attention = shifted / jnp.sum(shifted, axis=-1, keepdims=True)
    row_gate = row_mask[:, None, None, :, None]
    kept = attention.astype(jnp.bfloat16) * row_gate.astype(jnp.bfloat16)
    dweights = jnp.einsum(
        "btgrd,bjgd->bgrtj", cot_rows, value_rows, preferred_element_type=jnp.float32
    )
    row_delta = jnp.sum(attention * dweights, axis=-1, keepdims=True)
    dscore = (attention * (dweights - row_delta) * row_gate * HD ** (-0.5)).astype(jnp.bfloat16)
    key_grad = jnp.einsum(
        "bgrtj,btgrd->bjgd", dscore, query_rows, preferred_element_type=jnp.float32
    )
    value_grad = jnp.einsum("bgrtj,btgrd->bjgd", kept, cot_rows, preferred_element_type=jnp.float32)
    kv_grad = jnp.concatenate(
        [
            key_grad.reshape(flat_rows, key_value_columns),
            value_grad.reshape(flat_rows, key_value_columns),
        ],
        axis=1,
    ).astype(jnp.bfloat16)
    backward_piece = adapter_scale * jnp.concatenate(
        [
            lax.dot_general(
                kv_grad[:, :key_value_columns],
                adapter_up_weight[0, 0],
                contracted_columns,
                preferred_element_type=jnp.float32,
            ),
            lax.dot_general(
                kv_grad[:, key_value_columns:],
                adapter_up_weight[0, 1],
                contracted_columns,
                preferred_element_type=jnp.float32,
            ),
        ],
        axis=1,
    )
    backward_lowrank = lax.psum(backward_piece, "mp").astype(jnp.bfloat16)
    up_gradient = adapter_scale * jnp.stack(
        [
            lax.dot_general(
                lowrank_projection[:, :lowrank_state],
                kv_grad[:, :key_value_columns],
                contract_rows,
                preferred_element_type=jnp.float32,
            ),
            lax.dot_general(
                lowrank_projection[:, lowrank_state:],
                kv_grad[:, key_value_columns:],
                contract_rows,
                preferred_element_type=jnp.float32,
            ),
        ]
    )
    grad_down = lax.dot_general(
        image_fourth, backward_lowrank, contract_rows, preferred_element_type=jnp.float32
    )
    down_sum, up_sum = lax.psum((grad_down, up_gradient), "dp")
    image_gradient_total = lax.dot_general(
        kv_grad, full_weight, contracted_columns, preferred_element_type=jnp.float32
    )
    adapter_portion = lax.dot_general(
        backward_lowrank,
        adapter_down_weight[0],
        contracted_columns,
        preferred_element_type=jnp.float32,
    )
    current_layer = lax.dynamic_slice_in_dim(
        image_gradient_total, parallel_index * fourth_part, fourth_part, 1
    )
    image_gradient_total = lax.dynamic_update_slice_in_dim(
        image_gradient_total, current_layer + adapter_portion, parallel_index * fourth_part, 1
    )
    image_gradient_total = image_gradient_total.reshape(samples, image_rows, model_width)
    shared_sum = lax.psum_scatter(image_gradient_total, "segment", scatter_dimension=1, tiled=True)
    result = lax.psum(shared_sum, "mp")
    return (down_sum.astype(jnp.bfloat16)[None], up_sum.astype(jnp.bfloat16)[None], result)


def solution(mesh):
    in_specs = (
        P("dp", "segment", None),
        P("segment", "dp", None, "mp"),
        P("segment", "mp", None),
        P("segment", None, None, "mp"),
        P("segment", "dp", None, "mp"),
        P("segment", "dp", None, "mp"),
        P("dp"),
        P("dp"),
    )
    out_specs = (P("segment", "mp", None), P("segment", None, None, "mp"), P("dp", "segment", None))
    return jax.shard_map(body, mesh=mesh, in_specs=in_specs, out_specs=out_specs, check_vma=False)
```

profile of v0, /device:TPU:2, one launch (start us, length us, event | category | flops | bytes accessed | tf_op | source)
XLA Modules:
  0.0 390.2 jit_solution(4577795114373816345)
XLA Ops:
  7.2 0.7 all-gather.4.cloned.1.call-update
  8.0 0.7 all-gather.6.cloned.1.call-update
  10.0 1.3 copy.38
  11.3 2.0 copy.39
  13.4 88.8 %all-gather.4.cloned.1.call-done = bf16[1,128,8192]{2,1,0:T(8,128)(2,1)} async-done(((bf16[1,8,8192]{2,1,0:T(8,128)(2,1)}), bf16[1,128,8192]{2,1,0:T(8,128)(2,1)}) %all-gather.4.cloned.1.call-update) | async-done | bytes 2097168 | tf_op jit(solution)/shard_map/all_gather | solution.py:25
  102.2 1.3 fusion.21
  103.6 25.9 %psum.35 = bf16[128,128]{1,0:T(8,128)(2,1)S(1)} all-reduce(f32[128,128]{1,0:T(8,128)S(1)} %fusion.21), channel_id=1, replica_groups=mesh['segment'=16,'dp'=8,'mp'=4] {'mp'}, use_global_device_ids=true, to_apply=%region_0.0 | all-reduce | flops 16384 | bytes 98304 | tf_op jit(solution)/shard_map/psum | solution.py:34
  129.8 30.6 %all-gather.6.cloned.1.call-done = bf16[1,8192,2,256]{3,2,0,1:T(2,128)(2,1)} async-done(((bf16[1,1024,2,256]{3,2,0,1:T(2,128)(2,1)}), bf16[1,8192,2,256]{3,2,0,1:T(2,128)(2,1)}) %all-gather.6.cloned.1.call-update) | async-done | bytes 8388624 | tf_op jit(solution)/shard_map/all_gather | solution.py:53
  160.5 8.2 %copy.40 = bf16[1024,8,2,256]{3,1,2,0:T(8,128)(2,1)} copy(bf16[1024,8,2,256]{3,2,1,0:T(2,128)(2,1)} %bitcast.113) | data formatting | bytes 16777216
  168.6 4.6 %fusion.10 = bf16[128,512]{1,0:T(8,128)(2,1)S(1)} fusion(bf16[8192,512]{1,0:T(8,128)(2,1)} %bitcast.108, bf16[1,128,8192]{2,1,0:T(8,128)(2,1)S(1)} %copy-done.1, f32[128,256]{1,0:T(8,128)S(1)} %fusion.42, f32[128,256]{1,0:T(8,128)S(1)} %fusion.46), kind=kOutput, calls=%fused_computation.11 | convolution fusion | flops 1074003968 | bytes 10878976 | tf_op jit(solution)/shard_map/dot_general | solution.py:56
  173.3 0.3 fusion.66
  173.8 1.6 fusion.14
  175.6 0.3 multiply_reduce_fusion
  175.9 0.5 fusion.13
  176.4 1.5 slice-done.1
  177.9 4.8 %fusion.34 = f32[128,8192]{1,0:T(8,128)} fusion(bf16[8192,512]{1,0:T(8,128)(2,1)S(1)} %bitcast.111, bf16[128,256]{0,1:T(8,128)(2,1)S(1)} %bitcast.118, bf16[128,256]{0,1:T(8,128)(2,1)S(1)} %bitcast.120), kind=kOutput, calls=%fused_computation.42 | convolution fusion | flops 1074003968 | bytes 12713984 | tf_op jit(solution)/shard_map/dot_general | solution.py:135
  182.8 26.9 %psum.36 = bf16[128,128]{0,1:T(8,128)(2,1)S(1)} all-reduce(f32[128,128]{0,1:T(8,128)S(1)} %maximum_multiply_fusion.2), channel_id=1, replica_groups=mesh['segment'=16,'dp'=8,'mp'=4] {'mp'}, use_global_device_ids=true, to_apply=%region_4.5 | all-reduce | flops 16384 | bytes 98304 | tf_op jit(solution)/shard_map/psum | solution.py:114
  209.8 4.6 %copy.51 = f32[1,128,8192]{2,1,0:T(8,128)} copy(f32[1,128,8192]{2,1,0:T(8,128)} %bitcast.112) | data formatting | bytes 8388608
  214.3 2.5 fusion.1
  216.9 1.3 fusion.23
  218.7 89.1 %reduce-scatter.2.cloned.1.call-done = f32[1,8,8192]{2,1,0:T(8,128)} async-done(((f32[1,128,8192]{2,1,0:T(8,128)}), f32[1,8,8192]{2,1,0:T(8,128)}) %reduce-scatter.2.cloned.1.call-update) | async-done | bytes 262160 | tf_op jit(solution)/shard_map/reduce_scatter | solution.py:151
  307.7 52.3 %all-reduce.5 = (bf16[2048,128]{1,0:T(8,128)(2,1)}, bf16[2,64,256]{2,1,0:T(8,128)(2,1)}) all-reduce(f32[2048,128]{1,0:T(8,128)} %fusion.23, f32[2,64,256]{2,1,0:T(8,128)S(1)} %maximum_multiply_fusion.1), channel_id=1, replica_groups=mesh['segment'=16,'dp'=8,'mp'=4] {'dp'}, use_global_device_ids=true, to_apply=%region_5.6 | all-reduce | flops 294912 | bytes 1769472 | tf_op jit(solution)/shard_map/psum | solution.py:134
  360.0 22.0 %all-reduce.4.cloned.1.call-done = f32[1,8,8192]{2,1,0:T(8,128)} async-done(((f32[1,8,8192]{2,1,0:T(8,128)}), f32[1,8,8192]{2,1,0:T(8,128)}) %all-reduce.4.cloned.1.call-update) | async-done | bytes 262160 | tf_op jit(solution)/shard_map/psum | solution.py:152
  382.0 1.7 copy.57
  (32 shorter events, 1.5 us)
Async XLA Ops:
  7.2 95.1 %copy-start = (bf16[1,2048,128]{2,1,0:T(8,128)(2,1)S(1)}, bf16[1,2048,128]{2,1,0:T(8,128)(2,1)}, u32[]{:S(2)}) copy-start(bf16[1,2048,128]{2,1,0:T(8,128)(2,1)} %param.10) | copy-start | bytes 1572868
  7.2 122.3 %copy-start.3 = (bf16[1,2,64,256]{3,2,1,0:T(8,128)(2,1)S(1)}, bf16[1,2,64,256]{3,2,1,0:T(8,128)(2,1)}, u32[]{:S(2)}) copy-start(bf16[1,2,64,256]{3,2,1,0:T(8,128)(2,1)} %param.11) | copy-start | bytes 196612
  7.2 95.0 %all-gather.4.cloned.1.call-start = ((), (), s32[]{:S(2)}) async-start(), calls=%async_computation.1 | async-start | bytes 2228224 | tf_op jit(solution)/shard_map/all_gather | solution.py:25
  7.9 152.5 %all-gather.6.cloned.1.call-start = ((), (), s32[]{:S(2)}) async-start(), calls=%async_computation.4 | async-start | bytes 9437184 | tf_op jit(solution)/shard_map/all_gather | solution.py:53
  8.7 299.0 %reduce-scatter.2.cloned.1.call-start = ((), (), s32[]{:S(2)}) async-start(), calls=%async_computation.2 | async-start | bytes 4456448 | tf_op jit(solution)/shard_map/reduce_scatter | solution.py:151
  160.5 8.2 %copy-start.1 = (bf16[1,128,8192]{2,1,0:T(8,128)(2,1)S(1)}, bf16[1,128,8192]{2,1,0:T(8,128)(2,1)}, u32[]{:S(2)}) copy-start(bf16[1,128,8192]{2,1,0:T(8,128)(2,1)} %all-gather.4.cloned.1.call-done) | copy-start | bytes 6291460
  173.3 2.2 copy-start.2
  173.8 2.6 slice-start
  175.6 2.4 slice-start.1
  216.8 165.2 %all-reduce.4.cloned.1.call-start = ((), (), s32[]{:S(2)}) async-start(), calls=%async_computation.3 | async-start | bytes 524288 | tf_op jit(solution)/shard_map/psum | solution.py:152
Sparse Core Ops, SparseCore 0:
  10.1 92.1 all-gather.3
  104.4 56.0 all-gather.5
  217.0 90.7 reduce-scatter.1
  310.5 71.4 all-reduce.3
where the time goes:
time: 391 us; the launch traced here: 390 us
  waiting for transfers between devices  232 us (59%)
  blocking collectives  105 us (27%)
  local copies, waits for them, and re-layouts  19.3 us (5%)
  matrix products  18.3 us (5%)
  between operations  15.2 us (4%)
    reduce_scatter x1, waiting for transfers between devices, body(): lax.psum_scatter(image_gradient_total, 'segment', scatter_dimension=1, ti...  89.1 us
    all_gather x1, waiting for transfers between devices, body(): lax.all_gather(encoder_image_states, 'segment', axis=1, tiled=True)  88.8 us
    psum x1, blocking collectives, body(): down_sum, up_sum = lax.psum((grad_down, up_gradient), 'dp')  52.3 us
    all_gather x1, waiting for transfers between devices, body(): lax.all_gather(local_weight, 'dp', axis=0, tiled=True)  30.6 us
    psum x1, blocking collectives, body(): backward_lowrank = lax.psum(backward_piece, 'mp').astype(jnp.bfloat16)  26.9 us
    psum x1, blocking collectives, body(): lax.psum(jnp.dot(image_fourth, adapter_down_weight[0], preferred_element_...  25.9 us
    psum x1, waiting for transfers between devices, body(): result = lax.psum(shared_sum, 'mp')  22 us
    unnamed x15, local copies, waits for them, and re-layouts  15.9 us
  transfers between devices with their start and end apart: 4, of which 4 were waited for; matrix products, arithmetic and copies ran while one was open for 2% of the time, Pallas kernels for 0%

commit v1 on v0

--- a/solution.py
+++ b/solution.py
@@ -8,6 +8,37 @@
 adapter_scale = 2.0
 contract_rows = (((0,), (0,)), ((), ()))
 contracted_columns = (((1,), (1,)), ((), ()))
+
+
+def order_stages_all_over_axis(w_in, ndim_at):
+    parts_seen = []
+    n_now, latest, mat_out = (
+        jax.lax.axis_size("dp"),
+        jax.lax.axis_index("dp"),
+        w_in.shape[ndim_at],
+    )
+    for i0 in tuple(range(n_now)):
+        parts_seen.append((i0, (i0 + 1) % n_now))
+    sheets = []
+    for i0 in [*range(n_now)]:
+        sheets.append((i0, (i0 - 1) % n_now))
+    top = jnp.zeros(
+        (*w_in.shape[:ndim_at], n_now * mat_out, *w_in.shape[ndim_at + 1 :]), w_in.dtype
+    )
+    top = lax.dynamic_update_slice_in_dim(top, w_in, latest * mat_out, axis=ndim_at)
+    wide_out = main = w_in
+    b_next = n_now // 2
+    for w in tuple(range(1, b_next + 1)):
+        wide_out = jax.lax.ppermute(wide_out, "dp", parts_seen)
+        top = lax.dynamic_update_slice_in_dim(
+            top, wide_out, (latest - w) % n_now * mat_out, axis=ndim_at
+        )
+        if w < n_now - b_next:
+            main = jax.lax.ppermute(main, "dp", sheets)
+            top = lax.dynamic_update_slice_in_dim(
+                top, main, (latest + w) % n_now * mat_out, axis=ndim_at
+            )
+    return top
 
 
 def body(
@@ -50,7 +81,7 @@
         axis=1,
     )
     local_weight = frozen_key_value[0]
-    full_weight = lax.all_gather(local_weight, "dp", axis=0, tiled=True).reshape(
+    full_weight = order_stages_all_over_axis(local_weight, 0).reshape(
         model_width, 2 * key_value_columns
     )
     frozen_output = jnp.dot(flat_img, full_weight, preferred_element_type=jnp.float32)

time: 391 us -> 357 us (0.913)
  waiting for transfers between devices: 232 us -> 173 us
  local copies, waits for them, and re-layouts: 19.3 us -> 41.8 us
  starting transfers between devices: 0.16 us -> 9.1 us
  blocking collectives: 105 us -> 101 us
    all_gather x1, waiting for transfers between devices: 88.8 us -> 34.2 us  [body(): lax.all_gather(encoder_image_states, 'segment', axis=1, tiled=True)]
    all_gather x1 -> x0, waiting for transfers between devices: 30.6 us -> none  [body(): lax.all_gather(local_weight, 'dp', axis=0, tiled=True)]
    ppermute x0 -> x7, waiting for transfers between devices: none -> 25.2 us  [the longest x4 25.2 us: order_stages_all_over_axis(): wide_out = jax.lax.ppermute(wide_out, 'dp', parts_seen)]
    dynamic_update_slice x0 -> x8, local copies, waits for them, and re-layouts: none -> 17.4 us  [the longest x4 8.07 us: order_stages_all_over_axis(): lax.dynamic_update_slice_in_dim(top, wide_out, (latest - w) % n_now * mat...]
    ppermute x0 -> x7, starting transfers between devices: none -> 8.98 us  [the longest x3 8.96 us: order_stages_all_over_axis(): main = jax.lax.ppermute(main, 'dp', sheets)]
    broadcast_in_dim x0 -> x1, local copies, waits for them, and re-layouts: none -> 5.46 us  [order_stages_all_over_axis(): jnp.zeros((*w_in.shape[:ndim_at], n_now * mat_out, *w_in.shape[ndim_at +...]
    unnamed x15 -> x23, local copies, waits for them, and re-layouts: 15.9 us -> 15.6 us
  transfers between devices with their start and end apart: 4 -> 10, of which waited for: 4 -> 5; matrix products, arithmetic and copies ran while one was open for 2% -> 8% of each run, Pallas kernels for 0% -> 0%
where the time goes in v1:
time: 357 us
  waiting for transfers between devices  173 us (48%)
  blocking collectives  101 us (28%)
  local copies, waits for them, and re-layouts  41.8 us (12%)
  matrix products  16.7 us (5%)
  between operations  15.3 us (4%)
  starting transfers between devices  9.1 us (3%)
    reduce_scatter x1, waiting for transfers between devices, body(): lax.psum_scatter(image_gradient_total, 'segment', scatter_dimension=1, ti...  89.3 us
    psum x1, blocking collectives, body(): down_sum, up_sum = lax.psum((grad_down, up_gradient), 'dp')  51.2 us
    all_gather x1, waiting for transfers between devices, body(): lax.all_gather(encoder_image_states, 'segment', axis=1, tiled=True)  34.2 us
    psum x1, blocking collectives, body(): lax.psum(jnp.dot(image_fourth, adapter_down_weight[0], preferred_element_...  25.9 us
    ppermute x4, waiting for transfers between devices, order_stages_all_over_axis(): wide_out = jax.lax.ppermute(wide_out, 'dp', parts_seen)  25.2 us
    psum x1, blocking collectives, body(): backward_lowrank = lax.psum(backward_piece, 'mp').astype(jnp.bfloat16)  23.9 us
    psum x1, waiting for transfers between devices, body(): result = lax.psum(shared_sum, 'mp')  23.3 us
    unnamed x23, local copies, waits for them, and re-layouts  15.6 us
  transfers between devices with their start and end apart: 10, of which 5 were waited for; matrix products, arithmetic and copies ran while one was open for 8% of the time, Pallas kernels for 0%

profile of v1, /device:TPU:2, one launch (start us, length us, event | category | flops | bytes accessed | tf_op | source)
XLA Modules:
  0.0 356.8 jit_solution(10266128619672944551)
XLA Ops:
  8.0 2.9 collective-permute-start.1
  10.9 12.7 %collective-permute-done = bf16[1024,2,256]{2,1,0:T(2,128)(2,1)S(1)} collective-permute-done((bf16[1024,2,256]{2,1,0:T(2,128)(2,1)}, bf16[1024,2,256]{2,1,0:T(2,128)(2,1)S(1)}, u32[]{:S(2)}, u32[]{:S(2)}) %collective-permute-start) | collective-permute-done | bytes 1048608 | tf_op jit(solution)/shard_map/ppermute | solution.py:32
  23.6 3.1 collective-permute-start.3
  26.7 12.5 %collective-permute-done.2 = bf16[1024,2,256]{2,1,0:T(2,128)(2,1)} collective-permute-done((bf16[1024,2,256]{2,1,0:T(2,128)(2,1)S(1)}, bf16[1024,2,256]{2,1,0:T(2,128)(2,1)}, u32[]{:S(2)}, u32[]{:S(2)}) %collective-permute-start.2) | collective-permute-done | bytes 1048608 | tf_op jit(solution)/shard_map/ppermute | solution.py:32
  41.1 2.1 copy.34
  43.9 3.0 collective-permute-start.5
  46.9 5.5 %broadcast_in_dim.19 = bf16[8192,2,256]{2,1,0:T(2,128)(2,1)} broadcast(bf16[]{:T(256)} %constant.69.clone.1), dimensions={} | broadcast | bytes 8388610 | tf_op jit(solution)/shard_map/broadcast_in_dim | solution.py:25
  54.0 1.7 constant_dynamic-update-slice_fusion.6
  55.8 3.0 constant_dynamic-update-slice_fusion.5
  58.7 2.9 constant_dynamic-update-slice_fusion.4
  61.7 2.9 constant_dynamic-update-slice_fusion.3
  64.6 1.7 constant_dynamic-update-slice_fusion.2
  68.1 34.2 %all-gather.2.cloned.1.call-done = bf16[1,128,8192]{2,1,0:T(8,128)(2,1)} async-done(((bf16[1,8,8192]{2,1,0:T(8,128)(2,1)}), bf16[1,128,8192]{2,1,0:T(8,128)(2,1)}) %all-gather.2.cloned.1.call-update) | async-done | bytes 2097168 | tf_op jit(solution)/shard_map/all_gather | solution.py:56
  103.6 25.9 %psum.35 = bf16[128,128]{1,0:T(8,128)(2,1)S(1)} all-reduce(f32[128,128]{1,0:T(8,128)S(1)} %fusion.24), channel_id=1, replica_groups=mesh['segment'=16,'dp'=8,'mp'=4] {'mp'}, use_global_device_ids=true, to_apply=%region_0.0 | all-reduce | flops 16384 | bytes 98304 | tf_op jit(solution)/shard_map/psum | solution.py:65
  131.7 8.2 %copy.35 = bf16[1024,8,2,256]{3,1,2,0:T(8,128)(2,1)} copy(bf16[1024,8,2,256]{3,2,1,0:T(2,128)(2,1)} %bitcast.52) | data formatting | bytes 16777216
  139.8 5.8 %fusion.13 = bf16[128,512]{0,1:T(8,128)(2,1)S(1)} fusion(bf16[8192,512]{1,0:T(8,128)(2,1)} %bitcast.125, bf16[1,128,8192]{2,1,0:T(8,128)(2,1)S(1)} %copy-done.5, f32[128,256]{0,1:T(8,128)S(1)} %fusion.43, f32[128,256]{0,1:T(8,128)S(1)} %fusion.47), kind=kOutput, calls=%fused_computation.12 | convolution fusion | flops 1074003968 | bytes 10878976 | tf_op jit(solution)/shard_map/dot_general | solution.py:87
  149.7 2.8 fusion.37
  152.6 1.8 copy-done.1
  154.5 1.9 copy.46
  156.4 23.9 %psum.36 = bf16[128,128]{0,1:T(8,128)(2,1)S(1)} all-reduce(f32[128,128]{0,1:T(8,128)S(1)} %maximum_multiply_fusion.2), channel_id=1, replica_groups=mesh['segment'=16,'dp'=8,'mp'=4] {'mp'}, use_global_device_ids=true, to_apply=%region_4.5 | all-reduce | flops 16384 | bytes 98304 | tf_op jit(solution)/shard_map/psum | solution.py:145
  180.3 2.5 fusion.1
  184.8 89.3 %reduce-scatter.2.cloned.1.call-done = f32[1,8,8192]{2,1,0:T(8,128)} async-done(((f32[1,128,8192]{2,1,0:T(8,128)}), f32[1,8,8192]{2,1,0:T(8,128)}) %reduce-scatter.2.cloned.1.call-update) | async-done | bytes 262160 | tf_op jit(solution)/shard_map/reduce_scatter | solution.py:182
  274.1 51.2 %all-reduce.5 = (bf16[2048,128]{1,0:T(8,128)(2,1)}, bf16[2,64,256]{2,1,0:T(8,128)(2,1)}) all-reduce(f32[2048,128]{1,0:T(8,128)S(1)} %fusion.26, f32[2,64,256]{2,1,0:T(8,128)S(1)} %maximum_multiply_fusion.1), channel_id=1, replica_groups=mesh['segment'=16,'dp'=8,'mp'=4] {'dp'}, use_global_device_ids=true, to_apply=%region_5.6 | all-reduce | flops 294912 | bytes 1769472 | tf_op jit(solution)/shard_map/psum | solution.py:165
  325.3 23.3 %all-reduce.4.cloned.1.call-done = f32[1,8,8192]{2,1,0:T(8,128)} async-done(((f32[1,8,8192]{2,1,0:T(8,128)}), f32[1,8,8192]{2,1,0:T(8,128)}) %all-reduce.4.cloned.1.call-update) | async-done | bytes 262160 | tf_op jit(solution)/shard_map/psum | solution.py:183
  (58 shorter events, 16.6 us)
Async XLA Ops:
  7.2 95.1 %copy-start = (bf16[1,2048,128]{2,1,0:T(8,128)(2,1)S(1)}, bf16[1,2048,128]{2,1,0:T(8,128)(2,1)}, u32[]{:S(2)}) copy-start(bf16[1,2048,128]{2,1,0:T(8,128)(2,1)} %param.10) | copy-start | bytes 1572868
  7.2 45.2 %copy-start.2 = (bf16[1,1024,2,256]{3,2,1,0:T(2,128)(2,1)S(1)}, bf16[1,1024,2,256]{3,2,1,0:T(2,128)(2,1)}, u32[]{:S(2)}) copy-start(bf16[1,1024,2,256]{3,2,1,0:T(2,128)(2,1)} %param.9) | copy-start | bytes 3145732
  7.2 95.0 %all-gather.2.cloned.1.call-start = ((), (), s32[]{:S(2)}) async-start(), calls=%async_computation.1 | async-start | bytes 2228224 | tf_op jit(solution)/shard_map/all_gather | solution.py:56
  7.9 266.1 %reduce-scatter.2.cloned.1.call-start = ((), (), s32[]{:S(2)}) async-start(), calls=%async_computation.2 | async-start | bytes 4456448 | tf_op jit(solution)/shard_map/reduce_scatter | solution.py:182
  8.0 15.7 %collective-permute-start = (bf16[1024,2,256]{2,1,0:T(2,128)(2,1)}, bf16[1024,2,256]{2,1,0:T(2,128)(2,1)S(1)}, u32[]{:S(2)}, u32[]{:S(2)}) collective-permute-start(bf16[1024,2,256]{2,1,0:T(2,128)(2,1)} %bitcast.132), channel_id=1, source_target_pairs={{0,4},{4,8},{8,12},{12,16},{16,20},{20,24},{24,28},{28,0},{1,5},{5... | collective-permute-start | bytes 3145736 | tf_op jit(solution)/shard_map/ppermute | solution.py:32
  8.0 15.6 %collective-permute-start.1 = (bf16[1024,2,256]{2,1,0:T(2,128)(2,1)}, bf16[1024,2,256]{2,1,0:T(2,128)(2,1)}, u32[]{:S(2)}, u32[]{:S(2)}) collective-permute-start(bf16[1024,2,256]{2,1,0:T(2,128)(2,1)} %bitcast.133), channel_id=1, source_target_pairs={{0,28},{4,0},{8,4},{12,8},{16,12},{20,16},{24,20},{28,24},{1,29},{... | collective-permute-start | bytes 3145736 | tf_op jit(solution)/shard_map/ppermute | solution.py:37
  23.6 3.1 copy-start.3
  23.6 15.5 %collective-permute-start.2 = (bf16[1024,2,256]{2,1,0:T(2,128)(2,1)S(1)}, bf16[1024,2,256]{2,1,0:T(2,128)(2,1)}, u32[]{:S(2)}, u32[]{:S(2)}) collective-permute-start(bf16[1024,2,256]{2,1,0:T(2,128)(2,1)S(1)} %collective-permute-done), channel_id=1, source_target_pairs={{0,4},{4,8},{8,12},{12,16},{16,20},{20,24},{24,28},{28,0},{1,5},{5... | collective-permute-start | bytes 3145736 | tf_op jit(solution)/shard_map/ppermute | solution.py:32
  23.6 20.3 %collective-permute-start.3 = (bf16[1024,2,256]{2,1,0:T(2,128)(2,1)}, bf16[1024,2,256]{2,1,0:T(2,128)(2,1)}, u32[]{:S(2)}, u32[]{:S(2)}) collective-permute-start(bf16[1024,2,256]{2,1,0:T(2,128)(2,1)} %collective-permute-done.1), channel_id=1, source_target_pairs={{0,28},{4,0},{8,4},{12,8},{16,12},{20,16},{24,20},{28,24},{1,29},{... | collective-permute-start | bytes 3145736 | tf_op jit(solution)/shard_map/ppermute | solution.py:37
  39.2 22.5 %collective-permute-start.4 = (bf16[1024,2,256]{2,1,0:T(2,128)(2,1)}, bf16[1024,2,256]{2,1,0:T(2,128)(2,1)S(1)}, u32[]{:S(2)}, u32[]{:S(2)}) collective-permute-start(bf16[1024,2,256]{2,1,0:T(2,128)(2,1)} %collective-permute-done.2), channel_id=1, source_target_pairs={{0,4},{4,8},{8,12},{12,16},{16,20},{20,24},{24,28},{28,0},{1,5},{5... | collective-permute-start | bytes 3145736 | tf_op jit(solution)/shard_map/ppermute | solution.py:32
  43.9 10.2 %copy-start.4 = (bf16[1024,2,256]{2,1,0:T(2,128)(2,1)S(1)}, bf16[1024,2,256]{2,1,0:T(2,128)(2,1)}, u32[]{:S(2)}) copy-start(bf16[1024,2,256]{2,1,0:T(2,128)(2,1)} %copy-done.3) | copy-start | bytes 3145732
  43.9 22.4 %collective-permute-start.5 = (bf16[1024,2,256]{2,1,0:T(2,128)(2,1)}, bf16[1024,2,256]{2,1,0:T(2,128)(2,1)S(1)}, u32[]{:S(2)}, u32[]{:S(2)}) collective-permute-start(bf16[1024,2,256]{2,1,0:T(2,128)(2,1)} %collective-permute-done.3), channel_id=1, source_target_pairs={{0,28},{4,0},{8,4},{12,8},{16,12},{20,16},{24,20},{28,24},{1,29},{... | collective-permute-start | bytes 3145736 | tf_op jit(solution)/shard_map/ppermute | solution.py:37
  52.4 77.1 %copy-start.7 = (bf16[1,2,64,256]{3,2,1,0:T(8,128)(2,1)S(1)}, bf16[1,2,64,256]{3,2,1,0:T(8,128)(2,1)}, u32[]{:S(2)}) copy-start(bf16[1,2,64,256]{3,2,1,0:T(8,128)(2,1)} %param.11) | copy-start | bytes 196612
  61.7 68.3 %collective-permute-start.6 = (bf16[1024,2,256]{2,1,0:T(2,128)(2,1)S(1)}, bf16[1024,2,256]{2,1,0:T(2,128)(2,1)S(1)}, u32[]{:S(2)}, u32[]{:S(2)}) collective-permute-start(bf16[1024,2,256]{2,1,0:T(2,128)(2,1)S(1)} %collective-permute-done.4), channel_id=1, source_target_pairs={{0,4},{4,8},{8,12},{12,16},{16,20},{20,24},{24,28},{28,0},{1,5},{5... | collective-permute-start | bytes 3145736 | tf_op jit(solution)/shard_map/ppermute | solution.py:32
  131.7 8.2 %copy-start.5 = (bf16[1,128,8192]{2,1,0:T(8,128)(2,1)S(1)}, bf16[1,128,8192]{2,1,0:T(8,128)(2,1)}, u32[]{:S(2)}) copy-start(bf16[1,128,8192]{2,1,0:T(8,128)(2,1)} %all-gather.2.cloned.1.call-done) | copy-start | bytes 6291460
  139.8 6.4 %copy-start.6 = (bf16[1,1,128,2048]{2,3,1,0:T(8,128)(2,1)S(1)}, bf16[1,1,128,2048]{2,3,1,0:T(8,128)(2,1)}, u32[]{:S(2)}) copy-start(bf16[1,1,128,2048]{2,3,1,0:T(8,128)(2,1)} %copy.34) | copy-start | bytes 1572868
  146.1 2.2 slice-start
  146.6 3.0 slice-start.1
  152.5 2.0 copy-start.1
  182.9 165.7 %all-reduce.4.cloned.1.call-start = ((), (), s32[]{:S(2)}) async-start(), calls=%async_computation.3 | async-start | bytes 524288 | tf_op jit(solution)/shard_map/psum | solution.py:183
Sparse Core Ops, SparseCore 0:
  10.1 92.1 all-gather.1
  183.0 90.9 reduce-scatter.1
  277.0 71.5 all-reduce.3
